TPU v7x, 32 devices: a whole 2x2x4 slice. The times are simulated.
32 devices in a mesh: rows: 8 (over y, x, core), cols: 4 (over z).
Axes of the slice: x: 2, y: 2, z: 4, core: 2. Of those that a mesh axis runs over, the one named last changes fastest.
Arguments:
- panel: float32 [2048, 256], P(('rows', 'cols')), may hold values from -1 to 1, as said below
- trailing: float32 [2048, 2048], P('rows', 'cols'), may hold values from -6 to 6
Outputs:
- r_factor: float32 [256, 256], replicated
- coefficients: float32 [256, 2048], P(None, 'cols')
- updated: float32 [2048, 2048], P('rows', 'cols')
Inputs may be any that keep to these rules, and one draw needn't show every extreme that they name: panel has full column rank and is well conditioned; rows and columns carry different scales.
All inputs are finite; a program needn't handle non-finite values.
Results may differ from a plain program's by a relative error of at most 0.0003.
Values sent between devices are 32-bit elements; how exact they have to be, the bound alone decides.
No kernel may reach another device: no remote copies, remote signals or barrier semaphores. Data moves between devices by JAX's collectives and lax.ppermute only.
A program may use at most 64 MiB of HBM per device.

v0:
```python
import jax
import jax.numpy as jnp
from jax import lax
from jax.sharding import PartitionSpec as P


def product(left, right):
    return jnp.dot(left, right, precision=lax.Precision.HIGHEST)


def lower_inverse_of(lower):
    identity = jnp.eye(lower.shape[0], dtype=lower.dtype)
    return jax.scipy.linalg.solve_triangular(lower, identity, lower=True)


def cholesky_pair(matrix):
    lower = jnp.linalg.cholesky(matrix)
    return (lower, lower_inverse_of(lower))


def gram_of(matrix):
    return lax.dot_general(
        matrix, matrix, (((0,), (0,)), ((), ())), precision=lax.Precision.HIGHEST
    )


def cross_of(panel_block, trailing):
    return lax.dot_general(
        panel_block, trailing, (((0,), (0,)), ((), ())), precision=lax.Precision.HIGHEST
    )


def finish_early(lower_inverse, cross_terms, panel_block, trailing):
    coefficients = product(lower_inverse, cross_terms)
    mixing = product(lower_inverse.T, coefficients)
    updated = trailing - product(panel_block, mixing)
    return (coefficients, updated)


def local(panel, trailing):
    panel_block = lax.all_gather(panel, "cols", axis=0, tiled=True)
    width = panel_block.shape[1]
    stacked = jnp.concatenate([gram_of(panel_block), cross_of(panel_block, trailing)], axis=1)
    summed = lax.psum(stacked, "rows")
    lower, lower_inverse = cholesky_pair(summed[:, :width])
    r_upper = lower.T
    cross_joint = summed[:, width:]
    coefficients, updated = finish_early(lower_inverse, cross_joint, panel_block, trailing)
    return (r_upper, coefficients, updated)


def solution(mesh):
    return jax.shard_map(
        local,
        mesh=mesh,
        in_specs=(P(("rows", "cols"), None), P("rows", "cols")),
        out_specs=(P(), P(None, "cols"), P("rows", "cols")),
        check_vma=False,
    )
```

profile of v0, /device:TPU:0, one launch (start us, length us, event | category | flops | bytes accessed | tf_op | source)
XLA Modules:
  0.0 156.2 jit_solution(14104111784305048921)
XLA Ops:
  7.2 0.0 all-reduce.3.cloned.1.call-start
  7.2 16.0 %all_gather.3 = f32[256,256]{1,0:T(8,128)S(1)} all-gather(f32[64,256]{1,0:T(8,128)} %param.2), channel_id=1, replica_groups=mesh['rows'=8,'cols'=4] {'cols'}, dimensions={0}, use_global_device_ids=true | all-gather | bytes 327680 | tf_op jit(solution)/shard_map/all_gather | solution.py:41
  23.2 0.6 fusion.17
  23.8 1.0 fusion.18
  24.8 1.0 pad_maximum_fusion
  25.8 0.2 copy.7
  26.1 57.1 %all-reduce.3.cloned.1.call-done = f32[256,768]{0,1:T(8,128)} async-done(((f32[256,768]{0,1:T(8,128)}), f32[256,768]{0,1:T(8,128)}) %all-reduce.3.cloned.1.call-update) | async-done | bytes 786448 | tf_op jit(solution)/shard_map/psum | solution.py:44
  83.2 0.9 slice-done
  84.1 0.1 copy.6
  84.3 0.1 copy-done.2
  84.5 11.7 %cholesky.50 = f32[128,128]{1,0:T(8,128)S(1)} custom-call(f32[128,128]{1,0:T(8,128)S(1)} %cholesky.118), custom_call_target="Cholesky" | custom-call | tf_op jit(solution)/shard_map/jit(cholesky)/cholesky | solution.py:17
  96.2 9.8 %custom-call.15 = f32[1,128,128]{1,2,0:T(8,128)S(1)} custom-call(f32[1,128,128]{2,1,0:T(8,128)S(1)} %get-tuple-element.29), custom_call_target="InvertDiagBlocksLowerTriangular" | custom-call | tf_op jit(solution)/shard_map/jit(cholesky)/cholesky | solution.py:17
  106.0 0.2 constant_dynamic-update-slice_fusion.1
  106.3 0.3 convolution_subtract_fusion.1
  106.5 11.9 %cholesky.105 = f32[128,128]{1,0:T(8,128)S(1)} custom-call(f32[128,128]{1,0:T(8,128)S(1)} %convolution_subtract_fusion.1), custom_call_target="Cholesky" | custom-call | tf_op jit(solution)/shard_map/jit(cholesky)/cholesky | solution.py:17
  118.5 0.6 compare_reduce_fusion
  120.4 0.1 triangular_solve.44
  120.5 4.0 %while.1 = (s32[]{:T(128)}, f32[256,256]{1,0:T(8,128)S(1)}, s32[2,2]{1,0:T(2,128)S(1)}, f32[2,128,128]{2,1,0:T(8,128)S(1)}, s32[]{:T(128)}) while((s32[]{:T(128)}, f32[256,256]{1,0:T(8,128)S(1)}, s32[2,2]{1,0:T(2,128)S(1)}, f32[2,128,128]{2,1,0:T(8,128)S(1)}, s32[]{:T(128)}) %tuple.29), condition=%wide.while_cond, body=%wide.while_body.sunk | while | flops 2 | bytes 131181 | solution.py:13
  120.5 0.6 fusion.31
  121.1 1.4 bitcast_dynamic-update-slice_fusion.2
  122.5 0.6 fusion.31
  123.1 1.4 bitcast_dynamic-update-slice_fusion.2
  124.5 19.7 %custom-call.16 = f32[2,128,128]{1,2,0:T(8,128)S(1)} custom-call(f32[2,128,128]{2,1,0:T(8,128)S(1)} %get-tuple-element.10), custom_call_target="InvertDiagBlocksLowerTriangular" | custom-call | tf_op jit(solution)/shard_map/jit(_solve_triangular)/triangular_solve | solution.py:13
  144.2 0.3 fusion.7
  144.5 0.3 convolution_subtract_fusion
  144.7 0.3 fusion.10
  145.0 0.6 fusion.1
  145.7 0.6 fusion.6
  146.3 0.1 copy-done.1
  146.5 1.0 fusion
  147.5 1.0 copy.9
  148.5 0.8 copy.8
  (17 shorter events, 0.2 us)
Async XLA Ops:
  7.2 16.7 %copy-start = (f32[256,512]{1,0:T(8,128)S(1)}, f32[256,512]{1,0:T(8,128)}, u32[]{:S(2)}) copy-start(f32[256,512]{1,0:T(8,128)} %param.3) | copy-start | bytes 1572868
  7.2 76.0 %all-reduce.3.cloned.1.call-start = ((), (), s32[]{:S(2)}) async-start(), calls=%async_computation | async-start | bytes 1572864 | tf_op jit(solution)/shard_map/psum | solution.py:44
  83.2 0.9 slice-start
  83.2 1.2 copy-start.2
  145.7 0.8 copy-start.1
Sparse Core Ops, SparseCore 0:
  25.9 57.1 all-reduce.2
where the time goes:
time: 156 us
  waiting for transfers between devices  57.1 us (37%)
  other arithmetic  54.9 us (35%)
  blocking collectives  16 us (10%)
  between operations  15.5 us (10%)
  local copies, waits for them, and re-layouts  7.43 us (5%)
  matrix products  5.19 us (3%)
    psum x1, waiting for transfers between devices, local(): summed = lax.psum(stacked, 'rows')  57.1 us
    another operation x6, other arithmetic, cholesky_pair(): lower = jnp.linalg.cholesky(matrix)  34.1 us
    another operation x3, other arithmetic, lower_inverse_of(): return jax.scipy.linalg.solve_triangular(lower, identity, lower=True)  19.7 us
    all_gather x1, blocking collectives, local(): panel_block = lax.all_gather(panel, 'cols', axis=0, tiled=True)  16 us
    another operation x6, local copies, waits for them, and re-layouts  3.95 us
  transfers between devices with their start and end apart: 1, of which 1 were waited for; matrix products, arithmetic and copies ran while one was open for 0% of the time, Pallas kernels for 0%

commit v1 on v0

--- a/solution.py
+++ b/solution.py
@@ -41,7 +41,7 @@
     panel_block = lax.all_gather(panel, "cols", axis=0, tiled=True)
     width = panel_block.shape[1]
     stacked = jnp.concatenate([gram_of(panel_block), cross_of(panel_block, trailing)], axis=1)
-    summed = lax.psum(stacked, "rows")
+    summed = jnp.sum(lax.all_gather(stacked, "rows"), axis=0)
     lower, lower_inverse = cholesky_pair(summed[:, :width])
     r_upper = lower.T
     cross_joint = summed[:, width:]

time: 156 us -> 149 us (0.955)
  waiting for transfers between devices: 57.1 us -> 45.8 us
  other arithmetic: 54.9 us -> 58 us
    psum x1 -> x0, waiting for transfers between devices: 57.1 us -> none  [local(): summed = lax.psum(stacked, 'rows')]
    all_gather x0 -> x1, waiting for transfers between devices: none -> 45.8 us  [local(): summed = jnp.sum(lax.all_gather(stacked, 'rows'), axis=0)]
    reduce_sum x0 -> x1, other arithmetic: none -> 3.24 us  [local(): summed = jnp.sum(lax.all_gather(stacked, 'rows'), axis=0)]
    unnamed x9 -> x6, local copies, waits for them, and re-layouts: 2.31 us -> 3.21 us
  transfers between devices with their start and end apart: 1 -> 1, of which waited for: 1 -> 1; matrix products, arithmetic and copies ran while one was open for 0% -> 1% of each run, Pallas kernels for 0% -> 0%
where the time goes in v1:
time: 149 us; the launch traced here: 148 us
  other arithmetic  58 us (39%)
  waiting for transfers between devices  45.8 us (31%)
  blocking collectives  15.9 us (11%)
  between operations  15.5 us (10%)
  local copies, waits for them, and re-layouts  7.27 us (5%)
  matrix products  5.87 us (4%)
    all_gather x1, waiting for transfers between devices, local(): summed = jnp.sum(lax.all_gather(stacked, 'rows'), axis=0)  45.8 us
    another operation x6, other arithmetic, cholesky_pair(): lower = jnp.linalg.cholesky(matrix)  34.1 us
    another operation x3, other arithmetic, lower_inverse_of(): return jax.scipy.linalg.solve_triangular(lower, identity, lower=True)  19.7 us
    all_gather x1, blocking collectives, local(): panel_block = lax.all_gather(panel, 'cols', axis=0, tiled=True)  15.9 us
    another operation x6, local copies, waits for them, and re-layouts  3.95 us
    reduce_sum x1, other arithmetic, local(): summed = jnp.sum(lax.all_gather(stacked, 'rows'), axis=0)  3.24 us
    unnamed x6, local copies, waits for them, and re-layouts  3.21 us
  transfers between devices with their start and end apart: 1, of which 1 were waited for; matrix products, arithmetic and copies ran while one was open for 1% of the time, Pallas kernels for 0%

profile of v1, /device:TPU:0, one launch (start us, length us, event | category | flops | bytes accessed | tf_op | source)
XLA Modules:
  0.0 148.4 jit_solution(990278376439506469)
XLA Ops:
  7.2 0.0 all-gather.3.cloned.1.call-start
  7.2 15.9 %all_gather.9 = f32[256,256]{1,0:T(8,128)S(1)} all-gather(f32[64,256]{1,0:T(8,128)} %param.2), channel_id=1, replica_groups=mesh['rows'=8,'cols'=4] {'cols'}, dimensions={0}, use_global_device_ids=true | all-gather | bytes 327680 | tf_op jit(solution)/shard_map/all_gather | solution.py:41
  23.1 0.6 fusion.17
  23.7 1.7 %fusion.18 = f32[256,512]{1,0:T(8,128)S(1)} fusion(f32[256,256]{1,0:T(8,128)S(1)} %all_gather.9, f32[256,512]{1,0:T(8,128)} %param.3), kind=kOutput, calls=%fused_computation.41 | convolution fusion | flops 402653184 | bytes 1310720 | tf_op jit(solution)/shard_map/dot_general | solution.py:28
  25.4 0.9 pad_maximum_fusion
  26.3 0.0 all-gather.3.cloned.1.call-update
  26.3 1.2 copy.13
  27.6 45.8 %all-gather.3.cloned.1.call-done = f32[2048,768]{1,0:T(8,128)} async-done(((f32[256,768]{1,0:T(8,128)}), f32[2048,768]{1,0:T(8,128)}) %all-gather.3.cloned.1.call-update) | async-done | bytes 6291472 | tf_op jit(solution)/shard_map/all_gather | solution.py:44
  73.4 3.2 %reduce_sum.9 = f32[256,768]{1,0:T(8,128)S(1)} reduce(f32[8,256,768]{2,1,0:T(8,128)} %bitcast.45, f32[]{:T(128)} %constant.75.clone.1), dimensions={0}, to_apply=%region_0.0 | reduce | flops 1376256 | bytes 7077892 | tf_op jit(solution)/shard_map/reduce_sum | solution.py:44
  76.7 0.1 copy.17
  76.9 11.7 %cholesky.50 = f32[128,128]{1,0:T(8,128)S(1)} custom-call(f32[128,128]{1,0:T(8,128)S(1)} %cholesky.118), custom_call_target="Cholesky" | custom-call | tf_op jit(solution)/shard_map/jit(cholesky)/cholesky | solution.py:17
  88.6 9.8 %custom-call.15 = f32[1,128,128]{1,2,0:T(8,128)S(1)} custom-call(f32[1,128,128]{2,1,0:T(8,128)S(1)} %get-tuple-element.32), custom_call_target="InvertDiagBlocksLowerTriangular" | custom-call | tf_op jit(solution)/shard_map/jit(cholesky)/cholesky | solution.py:17
  98.5 0.2 constant_dynamic-update-slice_fusion.1
  98.7 0.3 convolution_subtract_fusion.1
  98.9 11.8 %cholesky.105 = f32[128,128]{1,0:T(8,128)S(1)} custom-call(f32[128,128]{1,0:T(8,128)S(1)} %convolution_subtract_fusion.1), custom_call_target="Cholesky" | custom-call | tf_op jit(solution)/shard_map/jit(cholesky)/cholesky | solution.py:17
  110.8 0.6 compare_reduce_fusion
  112.8 0.1 triangular_solve.44
  112.9 4.0 %while.1 = (s32[]{:T(128)}, f32[256,256]{1,0:T(8,128)S(1)}, s32[2,2]{1,0:T(2,128)S(1)}, f32[2,128,128]{2,1,0:T(8,128)S(1)}, s32[]{:T(128)}) while((s32[]{:T(128)}, f32[256,256]{1,0:T(8,128)S(1)}, s32[2,2]{1,0:T(2,128)S(1)}, f32[2,128,128]{2,1,0:T(8,128)S(1)}, s32[]{:T(128)}) %tuple.30), condition=%wide.while_cond, body=%wide.while_body.sunk | while | flops 2 | bytes 131181 | solution.py:13
  112.9 0.6 fusion.31
  113.5 1.4 bitcast_dynamic-update-slice_fusion.2
  114.9 0.6 fusion.31
  115.5 1.4 bitcast_dynamic-update-slice_fusion.2
  116.9 19.7 %custom-call.16 = f32[2,128,128]{1,2,0:T(8,128)S(1)} custom-call(f32[2,128,128]{2,1,0:T(8,128)S(1)} %get-tuple-element.10), custom_call_target="InvertDiagBlocksLowerTriangular" | custom-call | tf_op jit(solution)/shard_map/jit(_solve_triangular)/triangular_solve | solution.py:13
  136.6 0.3 fusion.7
  136.8 0.3 convolution_subtract_fusion
  137.1 0.3 fusion.10
  137.4 0.6 fusion.1
  138.1 0.0 copy-start
  138.1 0.6 fusion.6
  138.7 1.0 fusion
  139.8 1.0 copy.15
  140.8 0.8 copy.14
  (13 shorter events, 0.2 us)
Async XLA Ops:
  7.2 66.2 %all-gather.3.cloned.1.call-start = ((), (), s32[]{:S(2)}) async-start(), calls=%async_computation | async-start | bytes 7077888 | tf_op jit(solution)/shard_map/all_gather | solution.py:44
  138.1 3.5 %copy-start = (f32[256,512]{1,0:T(8,128)}, f32[256,512]{1,0:T(8,128)S(1)}, u32[]{:S(2)}) copy-start(f32[256,512]{1,0:T(8,128)S(1)} %fusion.1) | copy-start | bytes 1572868
Sparse Core Ops, SparseCore 0:
  26.4 46.9 all-gather.2
